TPU v7x, 32 devices: a whole 2x2x4 slice. The times are simulated.
32 devices in a mesh: groups: 2 (over x), context: 16 (over z, y, core).
Axes of the slice: x: 2, y: 2, z: 4, core: 2. Of those that a mesh axis runs over, the one named last changes fastest.
Arguments:
- encoded: bfloat16 [24576, 1536], P(('groups', 'context')), parts along dimension 0, may hold values from -64 to 64, as said below
- query_weight: bfloat16 [1536, 768], P('context'), may hold values from -0.104613624 to 0.104613624
- key_weight: bfloat16 [1536, 768], P('context'), may hold values from -4 to 4
- value_weight: bfloat16 [1536, 768], P('context'), may hold values from -0.15625 to 0.15625
- out_weight: bfloat16 [1536, 768], P('context'), may hold values from -0.875 to 0.875
- cotangent: bfloat16 [24576, 1536], P(('groups', 'context')), parts along dimension 0, may hold values from -6 to 6
- valid_frames: int32 [2], P('groups'), parts along dimension 0, may hold values from 11536 to 12288
Outputs:
- layer_out: bfloat16 [24576, 1536], P(('groups', 'context')), parts along dimension 0
- encoded_grad: bfloat16 [24576, 1536], P(('groups', 'context')), parts along dimension 0
- query_weight_grad: float32 [3072, 768], P(('groups', 'context')), parts along dimension 0
- key_weight_grad: float32 [3072, 768], P(('groups', 'context')), parts along dimension 0
- value_weight_grad: float32 [3072, 768], P(('groups', 'context')), parts along dimension 0
- out_weight_grad: float32 [3072, 768], P(('groups', 'context')), parts along dimension 0
There are 2 independent parts, one for each index of `groups`. A program takes and returns all parts, laid end to end along the dimension named above; an argument that names none is the same for every part. Nothing has to cross between parts.
Inputs may be any that keep to these rules, and one draw needn't show every extreme that they name: Frames at position valid_frames and later are padding. `encoded`: drawn afresh for each recording.
All inputs are finite; a program needn't handle non-finite values.
Results may differ from a plain program's by a relative error of at most 0.014.
The roundings to bfloat16 on the way count: a program that leaves them out, or rounds other values in their place, can miss the bound.
Values may be sent and summed in bfloat16 or wider, within the bound.
No kernel may reach another device: no remote copies, remote signals or barrier semaphores. Data moves between devices by JAX's collectives and lax.ppermute only.
A program may use at most 192 MiB of HBM per device.

v0:
```python
import jax
import jax.numpy as jnp
from jax import lax
from jax.sharding import PartitionSpec as P

HEADS = 12
HD = 64
BLOCK = 16
LEFT = 16
E = 768
epsilon = 1e-05


def passed_along(value, axis, by):
    count = lax.axis_size(axis)
    pairs = [(i, i + by) for i in range(count) if 0 <= i + by < count]
    return lax.ppermute(value, axis, pairs)


def normalize(encoded):
    values = encoded.astype(jnp.float32)
    centered = values - jnp.mean(values, axis=1, keepdims=True)
    inverse = lax.rsqrt(jnp.mean(centered * centered, axis=1, keepdims=True) + epsilon)
    return (centered * inverse, inverse)


def tile_probs(query_tile, key_tile, query_first, valid_count):
    span_rows = query_tile.shape[0]
    query_pos = query_first + jnp.arange(span_rows, dtype=jnp.int32)
    key_pos = query_first - span_rows + jnp.arange(2 * span_rows, dtype=jnp.int32)
    query_block = query_pos // BLOCK
    key_block = key_pos // BLOCK
    allowed = (key_pos[None, :] >= 0) & (key_pos[None, :] < valid_count)
    allowed = (
        allowed
        & (key_block[None, :] <= query_block[:, None])
        & (key_block[None, :] >= query_block[:, None] - LEFT)
    )
    scores = jnp.einsum(
        "qhd,khd->hqk",
        query_tile.reshape(span_rows, HEADS, HD),
        key_tile.reshape(2 * span_rows, HEADS, HD),
        preferred_element_type=jnp.float32,
    ) * HD ** (-0.5)
    scores = jnp.where(allowed[None], scores, -1e30)
    row_max = jnp.max(scores, axis=2, keepdims=True)
    shifted = jnp.exp(scores - row_max)
    return shifted / jnp.sum(shifted, axis=2, keepdims=True)


def shards(encoded, query_weight, key_weight, value_weight, out_weight, cotangent, valid_frames):
    valid_count = valid_frames[0]
    frames_dev = encoded.shape[0]
    span_rows = LEFT * BLOCK
    tile_total = frames_dev // span_rows
    first_row = lax.axis_index("context") * frames_dev
    row_mask = (first_row + jnp.arange(frames_dev, dtype=jnp.int32) < valid_count).astype(
        jnp.float32
    )[:, None]
    unit_rows, inverse = normalize(encoded)
    normed = unit_rows.astype(jnp.bfloat16)
    in_weights = jnp.concatenate([query_weight, key_weight, value_weight], axis=1)
    projected = jnp.dot(
        normed,
        lax.all_gather(in_weights, "context", axis=0, tiled=True),
        preferred_element_type=jnp.float32,
    )
    projected = projected.astype(jnp.bfloat16)
    queries = projected[:, :E]
    left_kv = passed_along(projected[frames_dev - span_rows :, E:], "context", 1)
    all_kv = jnp.concatenate([left_kv, projected[:, E:]], axis=0)
    prob_tiles = []
    low_tiles = []
    mixed_tiles = []
    for tile_id in range(tile_total):
        tile_start = tile_id * span_rows
        query_tile = queries[tile_start : tile_start + span_rows]
        kv_tile = all_kv[tile_start : tile_start + 2 * span_rows]
        attn_probs = tile_probs(query_tile, kv_tile[:, :E], first_row + tile_start, valid_count)
        probs_low = attn_probs.astype(jnp.bfloat16)
        value_tile = kv_tile[:, E:].reshape(2 * span_rows, HEADS, HD)
        mixed = jnp.einsum(
            "hqk,khd->qhd", probs_low, value_tile, preferred_element_type=jnp.float32
        )
        prob_tiles.append(attn_probs)
        low_tiles.append(probs_low)
        mixed_tiles.append(mixed.reshape(span_rows, E))
    attended = (jnp.concatenate(mixed_tiles, axis=0) * row_mask).astype(jnp.bfloat16)
    cotan_cols = cotangent
    out_grad_rows = lax.psum_scatter(
        jnp.einsum("fc,fe->ce", cotan_cols, attended, preferred_element_type=jnp.float32).astype(
            jnp.bfloat16
        ),
        "context",
        scatter_dimension=0,
        tiled=True,
    ).astype(jnp.float32)
    projected_out = jnp.einsum(
        "fe,de->fd",
        attended,
        lax.all_gather(out_weight, "context", axis=0, tiled=True),
        preferred_element_type=jnp.float32,
    )
    layer_out = (encoded.astype(jnp.float32) + projected_out).astype(jnp.bfloat16)
    cotan_cols = cotangent
    grad_attn = jnp.dot(
        cotan_cols,
        lax.all_gather(out_weight, "context", axis=0, tiled=True),
        preferred_element_type=jnp.float32,
    )
    grad_attn = (grad_attn * row_mask).astype(jnp.bfloat16)
    kv_back = jnp.zeros((frames_dev + span_rows, 2 * E), jnp.float32)
    query_tiles = []
    for tile_id in range(tile_total):
        tile_start = tile_id * span_rows
        query_tile = queries[tile_start : tile_start + span_rows].reshape(span_rows, HEADS, HD)
        kv_tile = all_kv[tile_start : tile_start + 2 * span_rows]
        key_tile = kv_tile[:, :E].reshape(2 * span_rows, HEADS, HD)
        value_tile = kv_tile[:, E:].reshape(2 * span_rows, HEADS, HD)
        grad_tile = grad_attn[tile_start : tile_start + span_rows].reshape(span_rows, HEADS, HD)
        attn_probs = prob_tiles[tile_id]
        prob_grad = jnp.einsum(
            "qhd,khd->hqk", grad_tile, value_tile, preferred_element_type=jnp.float32
        )
        row_delta = jnp.sum(attn_probs * prob_grad, axis=2, keepdims=True)
        score_grad = (attn_probs * (prob_grad - row_delta) * HD ** (-0.5)).astype(jnp.bfloat16)
        query_tiles.append(
            jnp.einsum(
                "hqk,khd->qhd", score_grad, key_tile, preferred_element_type=jnp.float32
            ).reshape(span_rows, E)
        )
        key_part = jnp.einsum(
            "hqk,qhd->khd", score_grad, query_tile, preferred_element_type=jnp.float32
        ).reshape(2 * span_rows, E)
        value_part = jnp.einsum(
            "hqk,qhd->khd", low_tiles[tile_id], grad_tile, preferred_element_type=jnp.float32
        ).reshape(2 * span_rows, E)
        kv_back = kv_back.at[tile_start : tile_start + 2 * span_rows].add(
            jnp.concatenate([key_part, value_part], axis=1)
        )
    returned = passed_along(kv_back[:span_rows].astype(jnp.bfloat16), "context", -1).astype(
        jnp.float32
    )
    own_back = kv_back[span_rows:].at[frames_dev - span_rows :].add(returned)
    back_rows = jnp.concatenate([jnp.concatenate(query_tiles, axis=0), own_back], axis=1).astype(
        jnp.bfloat16
    )
    in_grad_rows = lax.psum_scatter(
        jnp.einsum("fc,fe->ce", normed, back_rows, preferred_element_type=jnp.float32).astype(
            jnp.bfloat16
        ),
        "context",
        scatter_dimension=0,
        tiled=True,
    ).astype(jnp.float32)
    feature_grad = jnp.einsum(
        "fe,de->fd",
        back_rows,
        lax.all_gather(in_weights, "context", axis=0, tiled=True),
        preferred_element_type=jnp.float32,
    )
    centered_grad = (
        feature_grad
        - jnp.mean(feature_grad, axis=1, keepdims=True)
        - unit_rows * jnp.mean(feature_grad * unit_rows, axis=1, keepdims=True)
    )
    encoded_grad = (cotangent.astype(jnp.float32) + inverse * centered_grad).astype(jnp.bfloat16)
    return (
        layer_out,
        encoded_grad,
        in_grad_rows[:, :E],
        in_grad_rows[:, E : 2 * E],
        in_grad_rows[:, 2 * E : 3 * E],
        out_grad_rows,
    )


def solution(mesh):
    placed = (
        P(("groups", "context"), None),
        P("context", None),
        P("context", None),
        P("context", None),
        P("context", None),
        P(("groups", "context"), None),
        P("groups"),
    )
    return jax.shard_map(
        shards,
        mesh=mesh,
        in_specs=placed,
        out_specs=(
            P(("groups", "context"), None),
            P(("groups", "context"), None),
            P(("groups", "context"), None),
            P(("groups", "context"), None),
            P(("groups", "context"), None),
            P(("groups", "context"), None),
        ),
        check_vma=False,
    )
```

profile of v0, /device:TPU:0, one launch (start us, length us, event | category | flops | bytes accessed | tf_op | source)
XLA Modules:
  0.0 498.0 jit_solution(1828219959673834523)
XLA Ops:
  7.9 1.8 pad_maximum_fusion.5
  10.7 2.0 convert_reduce_fusion
  12.7 2.4 fusion.22
  17.7 37.5 %all-gather.5.cloned.1.call-done = bf16[1536,768]{1,0:T(8,128)(2,1)} async-done(((bf16[96,768]{1,0:T(8,128)(2,1)}), bf16[1536,768]{1,0:T(8,128)(2,1)}) %all-gather.5.cloned.1.call-update) | async-done | bytes 2359312 | tf_op jit(solution)/shard_map/all_gather | solution.py:101
  55.2 4.4 multiply_convert_fusion.3
  60.6 62.9 %all-gather.3.cloned.1.call-done = bf16[1536,2304]{1,0:T(8,128)(2,1)} async-done(((bf16[96,2304]{1,0:T(8,128)(2,1)}), bf16[1536,2304]{1,0:T(8,128)(2,1)}) %all-gather.3.cloned.1.call-update) | async-done | bytes 7077904 | tf_op jit(solution)/shard_map/all_gather | solution.py:65
  123.5 9.1 %convolution_convert_fusion.1 = bf16[768,2304]{1,0:T(8,128)(2,1)S(1)} fusion(bf16[1536,2304]{1,0:T(8,128)(2,1)} %all-gather.3.cloned.1.call-done, bf16[768,1536]{1,0:T(8,128)(2,1)S(1)} %copy-done.1, f32[768]{0:T(1024)S(1)} %add_rsqrt_fusion, f32[768]{0:T(1024)S(1)} %broadcast_multiply_fusion.2), kind=kOutput, calls=%fused_computation.32 | convolution fusion | flops 5442306048 | bytes 12982272 | tf_op jit(solution)/shard_map/dot_general | solution.py:63
  135.0 1.5 fusion.140
  136.5 1.9 copy.49
  138.5 2.3 copy.50
  140.8 2.3 copy.48
  143.1 6.8 %fusion.143 = (f32[12,256]{1,0:T(8,128)}, f32[12,256,512]{2,1,0:T(8,128)}) fusion(pred[256,512]{1,0:T(8,128)(4,1)} %compare_and_fusion, bf16[256,12,64]{0,2,1:T(8,128)(2,1)} %bitcast.117, bf16[512,12,64]{0,2,1:T(8,128)(2,1)} %bitcast.109), kind=kOutput, calls=%fused_computation.187 | convolution fusion | flops 207618560 | bytes 7614464 | tf_op jit(solution)/shard_map/sub | solution.py:47
  149.9 5.1 %fusion.69 = f32[12,64,256]{2,1,0:T(8,128)} fusion(bf16[512,12,64]{0,2,1:T(8,128)(2,1)} %bitcast.93, f32[12,256,512]{2,1,0:T(8,128)} %get-tuple-element.92, f32[12,256]{1,0:T(8,128)} %get-tuple-element.91), kind=kOutput, calls=%fused_computation.81 | convolution fusion | flops 204472320 | bytes 7876608 | tf_op jit(solution)/shard_map/hqk,khd->qhd/dot_general | solution.py:82
  155.0 1.9 fusion.67
  156.9 3.6 fusion.148
  160.5 3.3 collective-permute-start
  163.8 1.9 copy.43
  165.7 1.9 copy.46
  167.6 2.3 copy.47
  171.1 23.3 %fusion.43 = f32[12,64,512]{2,1,0:T(8,128)} fusion(bf16[256,12,64]{0,2,1:T(8,128)(2,1)} %bitcast.118, f32[12,256,512]{2,1,0:T(8,128)} %fusion.148, f32[12,256,512]{2,1,0:T(8,128)} %get-tuple-element.92, f32[12,256]{1,0:T(8,128)} %get-tuple-element.91), kind=kOutput, calls=%fused_computation.49 | convolution fusion | flops 212340224 | bytes 14561280 | tf_op jit(solution)/shard_map/hqk,qhd->khd/dot_general | solution.py:132
  194.4 4.7 fusion.147
  199.1 6.8 %fusion.144 = (f32[12,256]{1,0:T(8,128)}, f32[12,256,512]{2,1,0:T(8,128)}) fusion(pred[256,512]{1,0:T(8,128)(4,1)} %compare_and_fusion.1, bf16[256,12,64]{0,2,1:T(8,128)(2,1)} %bitcast.119, bf16[512,12,64]{0,2,1:T(8,128)(2,1)} %bitcast.111), kind=kOutput, calls=%fused_computation.188 | convolution fusion | flops 207618560 | bytes 7614464 | tf_op jit(solution)/shard_map/sub | solution.py:47
  205.9 4.9 fusion.73
  210.8 23.6 %fusion.37 = f32[12,64,512]{2,1,0:T(8,128)} fusion(bf16[256,12,64]{0,2,1:T(8,128)(2,1)} %bitcast.120, f32[12,256,512]{2,1,0:T(8,128)} %fusion.147, f32[12,256,512]{2,1,0:T(8,128)} %get-tuple-element.94, f32[12,256]{1,0:T(8,128)} %get-tuple-element.93), kind=kOutput, calls=%fused_computation.47 | convolution fusion | flops 212340224 | bytes 14561280 | tf_op jit(solution)/shard_map/hqk,qhd->khd/dot_general | solution.py:132
  234.5 4.9 fusion.71
  239.4 2.1 pad_maximum_fusion.1
  242.6 1.4 copy.42
  244.1 6.8 %fusion.145 = (f32[12,256]{1,0:T(8,128)}, f32[12,256,512]{2,1,0:T(8,128)}) fusion(pred[256,512]{1,0:T(8,128)(4,1)} %compare_and_fusion.2, bf16[256,12,64]{0,2,1:T(8,128)(2,1)} %bitcast.115, bf16[512,12,64]{0,2,1:T(8,128)(2,1)} %bitcast.113), kind=kOutput, calls=%fused_computation.189 | convolution fusion | flops 207618560 | bytes 7614464 | tf_op jit(solution)/shard_map/sub | solution.py:47
  250.9 5.0 fusion.77
  255.9 1.8 fusion.75
  257.7 3.6 fusion.146
  261.4 23.3 %fusion.31 = f32[12,64,512]{2,1,0:T(8,128)} fusion(bf16[256,12,64]{0,2,1:T(8,128)(2,1)} %bitcast.116, f32[12,256,512]{2,1,0:T(8,128)} %fusion.146, f32[12,256,512]{2,1,0:T(8,128)} %get-tuple-element.96, f32[12,256]{1,0:T(8,128)} %get-tuple-element.95), kind=kOutput, calls=%fused_computation.45 | convolution fusion | flops 212340224 | bytes 14561280 | tf_op jit(solution)/shard_map/hqk,qhd->khd/dot_general | solution.py:132
  284.6 5.5 %fusion.64 = bf16[1536,768]{0,1:T(8,128)(2,1)} fusion(bf16[768,1536]{1,0:T(8,128)(2,1)} %param.20, f32[256,768]{0,1:T(8,128)S(1)} %bitcast.121, f32[256,768]{0,1:T(8,128)} %bitcast.123, f32[256,768]{0,1:T(8,128)} %bitcast.125, f32[768]{0:T(1024)S(1)} %fusion.95), kind=kOutput, calls=%fused_computation.72 | convolution fusion | flops 1815478272 | bytes 7080960 | tf_op jit(solution)/shard_map/fc,fe->ce/dot_general | solution.py:91
  290.2 4.3 copy.52
  294.8 2.8 select_maximum_fusion
  299.6 2.9 constant_dynamic-update-slice_fusion
  302.5 2.6 copy-done
  307.4 25.0 %fusion.79 = bf16[12,64,256]{2,1,0:T(8,128)(2,1)S(1)} fusion(bf16[512,12,64]{0,2,1:T(8,128)(2,1)S(1)} %bitcast.110, f32[12,256,512]{2,1,0:T(8,128)} %fusion.148, f32[12,256,512]{2,1,0:T(8,128)} %get-tuple-element.92, f32[12,256]{1,0:T(8,128)} %get-tuple-element.91), kind=kOutput, calls=%fused_computation.91 | convolution fusion | flops 212536832 | bytes 13774848 | tf_op jit(solution)/shard_map/hqk,khd->qhd/dot_general | solution.py:128
  332.4 22.6 %fusion.82 = bf16[12,64,256]{2,1,0:T(8,128)(2,1)} fusion(bf16[512,12,64]{0,2,1:T(8,128)(2,1)} %bitcast.112, f32[12,256,512]{2,1,0:T(8,128)} %fusion.147, f32[12,256,512]{2,1,0:T(8,128)} %get-tuple-element.94, f32[12,256]{1,0:T(8,128)} %get-tuple-element.93), kind=kOutput, calls=%fused_computation.92 | convolution fusion | flops 212536832 | bytes 13774848 | tf_op jit(solution)/shard_map/hqk,khd->qhd/dot_general | solution.py:128
  355.0 4.0 slice.196
  359.0 25.7 %fusion.85 = bf16[12,64,256]{2,1,0:T(8,128)(2,1)} fusion(bf16[512,12,64]{0,2,1:T(8,128)(2,1)S(1)} %bitcast.114, f32[12,256,512]{2,1,0:T(8,128)} %fusion.146, f32[12,256,512]{2,1,0:T(8,128)} %get-tuple-element.96, f32[12,256]{1,0:T(8,128)} %get-tuple-element.95), kind=kOutput, calls=%fused_computation.93 | convolution fusion | flops 212536832 | bytes 13774848 | tf_op jit(solution)/shard_map/hqk,khd->qhd/dot_general | solution.py:128
  384.8 2.7 fusion.66
  387.5 11.0 %convolution_convert_fusion = bf16[1536,2304]{1,0:T(8,128)(2,1)} fusion(bf16[768,1536]{0,1:T(8,128)(2,1)} %fusion.66, bf16[256,768]{0,1:T(8,128)(2,1)S(1)} %bitcast.127, bf16[256,768]{0,1:T(8,128)(2,1)} %bitcast.129, bf16[256,768]{0,1:T(8,128)(2,1)} %bitcast.131, bf16[768,1536]{1,0:T(8,128)(2,1)S(1)} %copy-done.1, f32[768]{0:T(1024)S(1)} %add_rsqrt_fusion, ...), kind=kOutput, calls=%fused_computation.6 | convolution fusion | flops 5458231296 | bytes 12982272 | tf_op jit(solution)/shard_map/fc,fe->ce/dot_general | solution.py:149
  399.6 5.7 %fusion.23 = bf16[768,1536]{1,0:T(8,128)(2,1)} fusion(bf16[768,1536]{1,0:T(8,128)(2,1)S(1)} %copy-done.1, bf16[1536,768]{1,0:T(8,128)(2,1)} %all-gather.5.cloned.1.call-done, f32[256,768]{0,1:T(8,128)S(1)} %bitcast.122, f32[256,768]{0,1:T(8,128)} %bitcast.124, f32[256,768]{0,1:T(8,128)} %bitcast.126, f32[768]{0:T(1024)S(1)} %fusion.95), kind=kOutput, calls=%fused_computation.42 | convolution fusion | flops 1817837568 | bytes 9440256 | tf_op jit(solution)/shard_map/fe,de->fd/dot_general | solution.py:98
  405.3 10.9 %fusion.138 = (f32[768]{0:T(1024)S(1)}, f32[768]{0:T(1024)S(1)}, f32[768,1536]{1,0:T(8,128)S(1)}) fusion(f32[768]{0:T(1024)S(1)} %add_rsqrt_fusion, f32[768]{0:T(1024)S(1)} %broadcast_multiply_fusion.2, bf16[768,1536]{1,0:T(8,128)(2,1)S(1)} %copy-done.1, bf16[1536,2304]{1,0:T(8,128)(2,1)} %all-gather.3.cloned.1.call-done, ...), kind=kOutput, calls=%fused_computation.182 | convolution fusion | flops 5457049600 | bytes 17707008 | tf_op jit(solution)/shard_map/fe,de->fd/dot_general | solution.py:156
  416.3 2.8 fusion.21
  421.1 68.0 %reduce-scatter.5.cloned.1.call-done = bf16[96,2304]{1,0:T(8,128)(2,1)} async-done(((bf16[1536,2304]{1,0:T(8,128)(2,1)}), bf16[96,2304]{1,0:T(8,128)(2,1)}) %reduce-scatter.5.cloned.1.call-update) | async-done | bytes 442384 | tf_op jit(solution)/shard_map/reduce_scatter | solution.py:148
  489.1 2.0 fusion.142
  (86 shorter events, 16.8 us)
Async XLA Ops:
  7.2 48.1 %all-gather.5.cloned.1.call-start = ((), (), s32[]{:S(2)}) async-start(), calls=%async_computation.3 | async-start | bytes 2506752 | tf_op jit(solution)/shard_map/all_gather | solution.py:101
  7.9 115.6 %all-gather.3.cloned.1.call-start = ((), (), s32[]{:S(2)}) async-start(), calls=%async_computation.2 | async-start | bytes 7520256 | tf_op jit(solution)/shard_map/all_gather | solution.py:65
  9.8 409.3 %reduce-scatter.7.cloned.1.call-start = ((), (), s32[]{:S(2)}) async-start(), calls=%async_computation.5 | async-start | bytes 2506752
  17.7 105.8 %copy-start.1 = (bf16[768,1536]{1,0:T(8,128)(2,1)S(1)}, bf16[768,1536]{1,0:T(8,128)(2,1)}, u32[]{:S(2)}) copy-start(bf16[768,1536]{1,0:T(8,128)(2,1)} %param.15) | copy-start | bytes 7077892
  132.7 3.9 copy-start.2
  149.9 5.1 %copy-start.8 = (bf16[256,768]{0,1:T(8,128)(2,1)S(1)}, bf16[256,768]{0,1:T(8,128)(2,1)}, u32[]{:S(2)}) copy-start(bf16[256,768]{0,1:T(8,128)(2,1)} %get-tuple-element.85) | copy-start | bytes 1179652
  149.9 5.1 %copy-start.19 = (f32[12,256,512]{2,1,0:T(8,128)S(1)}, f32[12,256,512]{2,1,0:T(8,128)}, u32[]{:S(2)}) copy-start(f32[12,256,512]{2,1,0:T(8,128)} %get-tuple-element.92) | copy-start | bytes 18874372
  149.9 5.1 %copy-start.21 = (f32[12,256]{1,0:T(8,128)S(1)}, f32[12,256]{1,0:T(8,128)}, u32[]{:S(2)}) copy-start(f32[12,256]{1,0:T(8,128)} %get-tuple-element.91) | copy-start | bytes 36868
  155.0 1.9 copy-start.3
  160.5 78.9 %collective-permute-start = (bf16[256,1536]{1,0:T(8,128)(2,1)}, bf16[256,1536]{1,0:T(8,128)(2,1)}, u32[]{:S(2)}, u32[]{:S(2)}) collective-permute-start(bf16[256,1536]{1,0:T(8,128)(2,1)} %slice.182), channel_id=1, source_target_pairs={{0,1},{1,2},{2,3},{3,4},{4,5},{5,6},{6,7},{7,8},{8,9},{9,10},{10,1... | collective-permute-start | bytes 2359304 | tf_op jit(solution)/shard_map/ppermute | solution.py:17
  171.1 23.3 %copy-start.4 = (bf16[512,768]{0,1:T(8,128)(2,1)S(1)}, bf16[512,768]{0,1:T(8,128)(2,1)}, u32[]{:S(2)}) copy-start(bf16[512,768]{0,1:T(8,128)(2,1)} %copy.45) | copy-start | bytes 2359300
  210.8 23.6 %copy-start.7 = (bf16[256,768]{0,1:T(8,128)(2,1)S(1)}, bf16[256,768]{0,1:T(8,128)(2,1)}, u32[]{:S(2)}) copy-start(bf16[256,768]{0,1:T(8,128)(2,1)} %get-tuple-element.86) | copy-start | bytes 1179652
  210.8 23.7 %copy-start.22 = (f32[12,256]{1,0:T(8,128)S(1)}, f32[12,256]{1,0:T(8,128)}, u32[]{:S(2)}) copy-start(f32[12,256]{1,0:T(8,128)} %get-tuple-element.93) | copy-start | bytes 36868
  234.5 4.9 slice-start
  250.9 5.0 copy-start.20
  250.9 5.0 copy-start.23
  261.4 23.3 %copy-start.15 = (f32[12,64,256]{2,1,0:T(8,128)S(1)}, f32[12,64,256]{2,1,0:T(8,128)}, u32[]{:S(2)}) copy-start(f32[12,64,256]{2,1,0:T(8,128)} %fusion.69) | copy-start | bytes 2359300
  294.5 194.5 %reduce-scatter.5.cloned.1.call-start = ((), (), s32[]{:S(2)}) async-start(), calls=%async_computation.4 | async-start | bytes 7520256 | tf_op jit(solution)/shard_map/reduce_scatter | solution.py:148
  294.8 2.8 copy-start.11
  294.8 2.8 copy-start.12
  297.6 1.5 copy-start.9
  297.6 2.0 copy-start.10
  299.6 7.8 %copy-start.13 = (bf16[512,768]{0,1:T(8,128)(2,1)S(1)}, bf16[512,768]{0,1:T(8,128)(2,1)}, u32[]{:S(2)}) copy-start(bf16[512,768]{0,1:T(8,128)(2,1)} %copy.50) | copy-start | bytes 2359300
  302.5 2.6 copy-start
  306.1 78.7 %collective-permute-start.1 = (bf16[256,1536]{0,1:T(8,128)(2,1)}, bf16[256,1536]{0,1:T(8,128)(2,1)}, u32[]{:S(2)}, u32[]{:S(2)}) collective-permute-start(bf16[256,1536]{0,1:T(8,128)(2,1)} %slice.210), channel_id=1, source_target_pairs={{1,0},{2,1},{3,2},{4,3},{5,4},{6,5},{7,6},{8,7},{9,8},{10,9},{11,1... | collective-permute-start | bytes 2359304 | tf_op jit(solution)/shard_map/ppermute | solution.py:17
  332.4 26.7 %copy-start.14 = (bf16[512,768]{0,1:T(8,128)(2,1)S(1)}, bf16[512,768]{0,1:T(8,128)(2,1)}, u32[]{:S(2)}) copy-start(bf16[512,768]{0,1:T(8,128)(2,1)} %copy.44) | copy-start | bytes 2359300
  398.4 1.1 copy-start.16
  399.6 5.8 %copy-start.5 = (bf16[768,1536]{0,1:T(8,128)(2,1)S(1)}, bf16[768,1536]{0,1:T(8,128)(2,1)}, u32[]{:S(2)}) copy-start(bf16[768,1536]{0,1:T(8,128)(2,1)} %fusion.66) | copy-start | bytes 7077892
  399.6 5.8 %copy-start.17 = (bf16[12,64,256]{2,1,0:T(8,128)(2,1)S(1)}, bf16[12,64,256]{2,1,0:T(8,128)(2,1)}, u32[]{:S(2)}) copy-start(bf16[12,64,256]{2,1,0:T(8,128)(2,1)} %fusion.82) | copy-start | bytes 1179652
  399.6 5.8 %copy-start.18 = (bf16[12,64,256]{2,1,0:T(8,128)(2,1)S(1)}, bf16[12,64,256]{2,1,0:T(8,128)(2,1)}, u32[]{:S(2)}) copy-start(bf16[12,64,256]{2,1,0:T(8,128)(2,1)} %fusion.85) | copy-start | bytes 1179652
  405.3 11.0 %copy-start.6 = (bf16[768,1536]{1,0:T(8,128)(2,1)S(1)}, bf16[768,1536]{1,0:T(8,128)(2,1)}, u32[]{:S(2)}) copy-start(bf16[768,1536]{1,0:T(8,128)(2,1)} %param.20) | copy-start | bytes 7077892
Sparse Core Ops, SparseCore 0:
  10.3 44.9 all-gather.4
  58.1 65.3 all-gather.2
  294.7 62.3 reduce-scatter.6
  398.6 90.4 reduce-scatter.4
where the time goes:
time: 507 us; the launch traced here: 498 us
  matrix products  246 us (49%)
  waiting for transfers between devices  169 us (33%)
  local copies, waits for them, and re-layouts  39.2 us (8%)
  other arithmetic  23.3 us (5%)
  between operations  15.2 us (3%)
    dot_general x3, matrix products, shards(): jnp.einsum('hqk,khd->qhd', score_grad, key_tile, preferred_element_type=j...  73.4 us
    dot_general x3, matrix products, shards(): jnp.einsum('hqk,qhd->khd', score_grad, query_tile, preferred_element_type...  70.2 us
    reduce_scatter x1, waiting for transfers between devices, shards(): lax.psum_scatter(jnp.einsum('fc,fe->ce', normed, back_rows, preferred_ele...  68 us
    all_gather x1, waiting for transfers between devices, shards(): lax.all_gather(in_weights, 'context', axis=0, tiled=True)  62.9 us
    all_gather x1, waiting for transfers between devices, shards(): lax.all_gather(out_weight, 'context', axis=0, tiled=True)  37.5 us
    sub x3, matrix products, tile_probs(): shifted = jnp.exp(scores - row_max)  20.4 us
    dot_general x3, matrix products, shards(): jnp.einsum('hqk,khd->qhd', probs_low, value_tile, preferred_element_type=...  15 us
    dot_general x3, matrix products, shards(): jnp.einsum('qhd,khd->hqk', grad_tile, value_tile, preferred_element_type=...  12 us
  transfers between devices with their start and end apart: 6, of which 3 were waited for; matrix products, arithmetic and copies ran while one was open for 42% of the time, Pallas kernels for 0%

commit v1 on v0

--- a/solution.py
+++ b/solution.py
@@ -9,6 +9,14 @@
 LEFT = 16
 E = 768
 epsilon = 1e-05
+
+
+def watch_the_copies(page, along_dim):
+    page = jnp.moveaxis(page, 0, along_dim)
+    earlier = page.shape
+    return page.reshape(
+        *earlier[:along_dim], earlier[along_dim] * earlier[along_dim + 1], *earlier[along_dim + 2 :]
+    )
 
 
 def passed_along(value, axis, by):
@@ -49,6 +57,28 @@
 
 
 def shards(encoded, query_weight, key_weight, value_weight, out_weight, cotangent, valid_frames):
+
+    def serve_digits(my_tile, mesh_dim, d0):
+        axis_len = lax.axis_size(mesh_dim)
+        trail = [(src_i, (src_i + 1) % axis_len) for src_i in range(axis_len)]
+        store = [(ix, no) for no, ix in trail]
+        left_arr, outcome_arr = ([], [])
+        q = 0
+        while q < axis_len - 1:
+            if q % 2 == 0:
+                left_arr.append(
+                    lax.ppermute(left_arr[-1] if left_arr else my_tile, mesh_dim, trail)
+                )
+            else:
+                outcome_arr.append(
+                    lax.ppermute(outcome_arr[-1] if outcome_arr else my_tile, mesh_dim, store)
+                )
+            q = q + 1
+        part_now = jnp.stack([*left_arr[::-1], my_tile, *outcome_arr])
+        opened = lax.axis_index(mesh_dim) - len(left_arr)
+        part_now = part_now[(jnp.arange(axis_len) - opened) % axis_len]
+        return watch_the_copies(part_now, d0)
+
     valid_count = valid_frames[0]
     frames_dev = encoded.shape[0]
     span_rows = LEFT * BLOCK
@@ -61,9 +91,7 @@
     normed = unit_rows.astype(jnp.bfloat16)
     in_weights = jnp.concatenate([query_weight, key_weight, value_weight], axis=1)
     projected = jnp.dot(
-        normed,
-        lax.all_gather(in_weights, "context", axis=0, tiled=True),
-        preferred_element_type=jnp.float32,
+        normed, serve_digits(in_weights, "context", 0), preferred_element_type=jnp.float32
     )
     projected = projected.astype(jnp.bfloat16)
     queries = projected[:, :E]

time: 507 us -> 510 us (level)
  waiting for transfers between devices: 169 us -> 117 us
  starting transfers between devices: 4.9 us -> 50.8 us
  local copies, waits for them, and re-layouts: 39.2 us -> 57.3 us
    all_gather x1, waiting for transfers between devices: 62.9 us -> 0.01 us  [shards(): lax.all_gather(in_weights, 'context', axis=0, tiled=True)]
    ppermute x0 -> x15, waiting for transfers between devices: none -> 45.9 us  [the longest x8 45.8 us: serve_digits(): lax.ppermute(left_arr[-1] if left_arr else my_tile, mesh_dim, trail)]
    ppermute x0 -> x15, starting transfers between devices: none -> 38.5 us  [the longest x8 20.1 us: serve_digits(): lax.ppermute(left_arr[-1] if left_arr else my_tile, mesh_dim, trail)]
    all_gather x1, waiting for transfers between devices: 37.5 us -> 0.02 us  [shards(): lax.all_gather(out_weight, 'context', axis=0, tiled=True)]
    unnamed x51 -> x72, local copies, waits for them, and re-layouts: 11 us -> 22.4 us
    ppermute x2, starting transfers between devices: 4.57 us -> 12.2 us  [passed_along(): return lax.ppermute(value, axis, pairs)]
    gather x0 -> x1, local copies, waits for them, and re-layouts: none -> 7.11 us  [serve_digits(): part_now = part_now[(jnp.arange(axis_len) - opened) % axis_len]]
  transfers between devices with their start and end apart: 6 -> 21, of which waited for: 3 -> 9; matrix products, arithmetic and copies ran while one was open for 42% -> 62% of each run, Pallas kernels for 0% -> 0%
where the time goes in v1:
time: 510 us; the launch traced here: 504 us
  matrix products  244 us (48%)
  waiting for transfers between devices  117 us (23%)
  local copies, waits for them, and re-layouts  57.3 us (11%)
  starting transfers between devices  50.8 us (10%)
  other arithmetic  19.7 us (4%)
  between operations  15.1 us (3%)
    dot_general x3, matrix products, shards(): jnp.einsum('hqk,khd->qhd', score_grad, key_tile, preferred_element_type=j...  73.4 us
    dot_general x3, matrix products, shards(): jnp.einsum('hqk,qhd->khd', score_grad, query_tile, preferred_element_type...  70.4 us
    reduce_scatter x1, waiting for transfers between devices, shards(): lax.psum_scatter(jnp.einsum('fc,fe->ce', normed, back_rows, preferred_ele...  70.1 us
    ppermute x8, waiting for transfers between devices, serve_digits(): lax.ppermute(left_arr[-1] if left_arr else my_tile, mesh_dim, trail)  45.8 us
    unnamed x72, local copies, waits for them, and re-layouts  22.4 us
    sub x3, matrix products, tile_probs(): shifted = jnp.exp(scores - row_max)  20.1 us
    ppermute x8, starting transfers between devices, serve_digits(): lax.ppermute(left_arr[-1] if left_arr else my_tile, mesh_dim, trail)  20.1 us
    ppermute x7, starting transfers between devices, serve_digits(): lax.ppermute(outcome_arr[-1] if outcome_arr else my_tile, mesh_dim, store)  18.4 us
  transfers between devices with their start and end apart: 21, of which 9 were waited for; matrix products, arithmetic and copies ran while one was open for 62% of the time, Pallas kernels for 0%

profile of v1, /device:TPU:0, one launch (start us, length us, event | category | flops | bytes accessed | tf_op | source)
XLA Modules:
  0.0 503.6 jit_solution(8810971154490134376)
XLA Ops:
  10.5 11.0 %collective-permute-done = bf16[96,2304]{1,0:T(8,128)(2,1)S(1)} collective-permute-done((bf16[96,2304]{1,0:T(8,128)(2,1)S(1)}, bf16[96,2304]{1,0:T(8,128)(2,1)S(1)}, u32[]{:S(2)}, u32[]{:S(2)}) %collective-permute-start) | collective-permute-done | bytes 442400 | tf_op jit(solution)/shard_map/ppermute | solution.py:70
  21.5 4.4 collective-permute-start.8
  26.7 5.3 %collective-permute-done.1 = bf16[96,2304]{1,0:T(8,128)(2,1)S(1)} collective-permute-done((bf16[96,2304]{1,0:T(8,128)(2,1)S(1)}, bf16[96,2304]{1,0:T(8,128)(2,1)S(1)}, u32[]{:S(2)}, u32[]{:S(2)}) %collective-permute-start.1) | collective-permute-done | bytes 442400 | tf_op jit(solution)/shard_map/ppermute | solution.py:70
  32.1 4.5 collective-permute-start.9
  36.6 10.1 %collective-permute-done.2 = bf16[96,2304]{1,0:T(8,128)(2,1)S(1)} collective-permute-done((bf16[96,2304]{1,0:T(8,128)(2,1)S(1)}, bf16[96,2304]{1,0:T(8,128)(2,1)S(1)}, u32[]{:S(2)}, u32[]{:S(2)}) %collective-permute-start.2) | collective-permute-done | bytes 442400 | tf_op jit(solution)/shard_map/ppermute | solution.py:70
  46.8 4.5 collective-permute-start.10
  51.2 6.2 %collective-permute-done.3 = bf16[96,2304]{1,0:T(8,128)(2,1)S(1)} collective-permute-done((bf16[96,2304]{1,0:T(8,128)(2,1)S(1)}, bf16[96,2304]{1,0:T(8,128)(2,1)S(1)}, u32[]{:S(2)}, u32[]{:S(2)}) %collective-permute-start.3) | collective-permute-done | bytes 442400 | tf_op jit(solution)/shard_map/ppermute | solution.py:70
  57.4 4.3 collective-permute-start.4
  65.6 2.8 collective-permute-done.4
  68.4 4.5 collective-permute-start.5
  73.7 3.8 collective-permute-start.12
  77.6 3.5 collective-permute-done.5
  81.0 4.4 collective-permute-start.6
  85.4 2.4 fusion.22
  88.1 3.4 collective-permute-done.6
  91.5 6.4 %collective-permute-start.7 = (bf16[96,2304]{1,0:T(8,128)(2,1)S(1)}, bf16[96,2304]{1,0:T(8,128)(2,1)S(1)}, u32[]{:S(2)}, u32[]{:S(2)}) collective-permute-start(bf16[96,2304]{1,0:T(8,128)(2,1)S(1)} %collective-permute-done.6), channel_id=1, source_target_pairs={{0,1},{1,2},{2,3},{3,4},{4,5},{5,6},{6,7},{7,8},{8,9},{9,10},{10,1... | collective-permute-start | bytes 1327112 | tf_op jit(solution)/shard_map/ppermute | solution.py:70
  98.7 3.6 collective-permute-done.7
  115.2 7.1 %gather_fusion = bf16[16,96,2304]{2,1,0:T(8,128)(2,1)} fusion(bf16[16,96,2304]{2,1,0:T(8,128)(2,1)} %bitcast_dynamic-update-slice_fusion, s32[1024]{0:T(1024)S(1)} %pad_clamp_fusion), kind=kCustom, calls=%fused_computation | custom fusion | bytes 14155840 | tf_op jit(solution)/shard_map/gather | solution.py:79
  122.3 9.1 %convolution_convert_fusion.1 = bf16[768,2304]{1,0:T(8,128)(2,1)S(1)} fusion(bf16[1536,2304]{1,0:T(8,128)(2,1)} %bitcast.126, bf16[768,1536]{1,0:T(8,128)(2,1)S(1)} %copy-done, f32[768]{0:T(1024)S(1)} %add_rsqrt_fusion, f32[768]{0:T(1024)S(1)} %broadcast_multiply_fusion.2), kind=kOutput, calls=%fused_computation.33 | convolution fusion | flops 5442306048 | bytes 12982272 | tf_op jit(solution)/shard_map/dot_general | solution.py:93
  135.2 10.9 %collective-permute-start.15 = (bf16[256,1536]{1,0:T(8,128)(2,1)}, bf16[256,1536]{1,0:T(8,128)(2,1)}, u32[]{:S(2)}, u32[]{:S(2)}) collective-permute-start(bf16[256,1536]{1,0:T(8,128)(2,1)} %slice.184), channel_id=1, source_target_pairs={{0,1},{1,2},{2,3},{3,4},{4,5},{5,6},{6,7},{7,8},{8,9},{9,10},{10,1... | collective-permute-start | bytes 2359304 | tf_op jit(solution)/shard_map/ppermute | solution.py:25
  158.1 6.7 %fusion.145 = (f32[12,256]{1,0:T(8,128)}, f32[12,256,512]{2,1,0:T(8,128)}) fusion(pred[256,512]{1,0:T(8,128)(4,1)} %compare_and_fusion, bf16[256,12,64]{0,2,1:T(8,128)(2,1)} %bitcast.155, bf16[512,12,64]{0,2,1:T(8,128)(2,1)} %bitcast.147), kind=kOutput, calls=%fused_computation.213 | convolution fusion | flops 207618560 | bytes 7614464 | tf_op jit(solution)/shard_map/sub | solution.py:55
  164.8 6.7 %fusion.146 = (f32[12,256]{1,0:T(8,128)}, f32[12,256,512]{2,1,0:T(8,128)}) fusion(pred[256,512]{1,0:T(8,128)(4,1)} %compare_and_fusion.1, bf16[256,12,64]{0,2,1:T(8,128)(2,1)S(1)} %bitcast.154, bf16[512,12,64]{0,2,1:T(8,128)(2,1)} %bitcast.145), kind=kOutput, calls=%fused_computation.214 | convolution fusion | flops 207618560 | bytes 7614464 | tf_op jit(solution)/shard_map/sub | solution.py:55
  171.5 5.2 %fusion.69 = f32[12,64,256]{2,1,0:T(8,128)} fusion(bf16[512,12,64]{0,2,1:T(8,128)(2,1)} %bitcast.129, f32[12,256,512]{2,1,0:T(8,128)} %get-tuple-element.92, f32[12,256]{1,0:T(8,128)} %get-tuple-element.91), kind=kOutput, calls=%fused_computation.82 | convolution fusion | flops 204472320 | bytes 7876608 | tf_op jit(solution)/shard_map/hqk,khd->qhd/dot_general | solution.py:110
  176.7 2.4 fusion.73
  179.1 2.4 pad_maximum_fusion.1
  186.1 6.7 %fusion.147 = (f32[12,256]{1,0:T(8,128)}, f32[12,256,512]{2,1,0:T(8,128)}) fusion(pred[256,512]{1,0:T(8,128)(4,1)} %compare_and_fusion.2, bf16[256,12,64]{0,2,1:T(8,128)(2,1)S(1)} %bitcast.152, bf16[512,12,64]{0,2,1:T(8,128)(2,1)} %bitcast.149), kind=kOutput, calls=%fused_computation.215 | convolution fusion | flops 207618560 | bytes 7614464 | tf_op jit(solution)/shard_map/sub | solution.py:55
  192.8 4.0 fusion.77
  197.7 3.4 fusion.64
  201.1 4.3 copy.52
  206.3 4.5 multiply_convert_fusion.3
  211.7 3.6 fusion.150
  215.4 23.8 %fusion.43 = f32[12,64,512]{2,1,0:T(8,128)} fusion(bf16[256,12,64]{0,2,1:T(8,128)(2,1)} %bitcast.156, f32[12,256,512]{2,1,0:T(8,128)} %fusion.150, f32[12,256,512]{2,1,0:T(8,128)} %get-tuple-element.92, f32[12,256]{1,0:T(8,128)} %get-tuple-element.91), kind=kOutput, calls=%fused_computation.50 | convolution fusion | flops 212340224 | bytes 14561280 | tf_op jit(solution)/shard_map/hqk,qhd->khd/dot_general | solution.py:160
  239.2 5.0 fusion.148
  244.2 23.3 %fusion.31 = f32[12,64,512]{2,1,0:T(8,128)} fusion(bf16[256,12,64]{0,2,1:T(8,128)(2,1)} %bitcast.151, f32[12,256,512]{2,1,0:T(8,128)} %fusion.148, f32[12,256,512]{2,1,0:T(8,128)} %get-tuple-element.96, f32[12,256]{1,0:T(8,128)} %get-tuple-element.95), kind=kOutput, calls=%fused_computation.46 | convolution fusion | flops 212340224 | bytes 14561280 | tf_op jit(solution)/shard_map/hqk,qhd->khd/dot_general | solution.py:160
  267.5 4.7 fusion.149
  272.2 23.2 %fusion.37 = f32[12,64,512]{2,1,0:T(8,128)} fusion(bf16[256,12,64]{0,2,1:T(8,128)(2,1)} %bitcast.153, f32[12,256,512]{2,1,0:T(8,128)} %fusion.149, f32[12,256,512]{2,1,0:T(8,128)} %get-tuple-element.94, f32[12,256]{1,0:T(8,128)} %get-tuple-element.93), kind=kOutput, calls=%fused_computation.48 | convolution fusion | flops 212340224 | bytes 14561280 | tf_op jit(solution)/shard_map/hqk,qhd->khd/dot_general | solution.py:160
  295.5 3.4 fusion.75
  300.0 4.8 fusion.71
  307.5 2.9 constant_dynamic-update-slice_fusion.3
  314.4 24.9 %fusion.79 = bf16[12,64,256]{2,1,0:T(8,128)(2,1)S(1)} fusion(bf16[512,12,64]{0,2,1:T(8,128)(2,1)S(1)} %bitcast.148, f32[12,256,512]{2,1,0:T(8,128)} %fusion.150, f32[12,256,512]{2,1,0:T(8,128)} %get-tuple-element.92, f32[12,256]{1,0:T(8,128)} %get-tuple-element.91), kind=kOutput, calls=%fused_computation.92 | convolution fusion | flops 212536832 | bytes 13774848 | tf_op jit(solution)/shard_map/hqk,khd->qhd/dot_general | solution.py:156
  339.3 22.7 %fusion.85 = bf16[12,64,256]{2,1,0:T(8,128)(2,1)} fusion(bf16[512,12,64]{0,2,1:T(8,128)(2,1)} %bitcast.150, f32[12,256,512]{2,1,0:T(8,128)} %fusion.148, f32[12,256,512]{2,1,0:T(8,128)} %get-tuple-element.96, f32[12,256]{1,0:T(8,128)} %get-tuple-element.95), kind=kOutput, calls=%fused_computation.94 | convolution fusion | flops 212536832 | bytes 13774848 | tf_op jit(solution)/shard_map/hqk,khd->qhd/dot_general | solution.py:156
  362.1 25.7 %fusion.82 = bf16[12,64,256]{2,1,0:T(8,128)(2,1)} fusion(bf16[512,12,64]{0,2,1:T(8,128)(2,1)S(1)} %bitcast.146, f32[12,256,512]{2,1,0:T(8,128)} %fusion.149, f32[12,256,512]{2,1,0:T(8,128)} %get-tuple-element.94, f32[12,256]{1,0:T(8,128)} %get-tuple-element.93), kind=kOutput, calls=%fused_computation.93 | convolution fusion | flops 212536832 | bytes 13774848 | tf_op jit(solution)/shard_map/hqk,khd->qhd/dot_general | solution.py:156
  387.8 2.7 fusion.66
  390.5 11.0 %convolution_convert_fusion = bf16[1536,2304]{1,0:T(8,128)(2,1)} fusion(bf16[768,1536]{0,1:T(8,128)(2,1)} %fusion.66, bf16[256,768]{0,1:T(8,128)(2,1)S(1)} %bitcast.163, bf16[256,768]{0,1:T(8,128)(2,1)} %bitcast.167, bf16[256,768]{0,1:T(8,128)(2,1)} %bitcast.165, bf16[768,1536]{1,0:T(8,128)(2,1)S(1)} %copy-done, f32[768]{0:T(1024)S(1)} %add_rsqrt_fusion, ...), kind=kOutput, calls=%fused_computation.7 | convolution fusion | flops 5458231296 | bytes 12982272 | tf_op jit(solution)/shard_map/fc,fe->ce/dot_general | solution.py:177
  402.6 5.6 %fusion.23 = bf16[768,1536]{1,0:T(8,128)(2,1)} fusion(bf16[768,1536]{1,0:T(8,128)(2,1)S(1)} %copy-done, bf16[1536,768]{1,0:T(8,128)(2,1)} %all-gather.3.cloned.1.call-done, f32[256,768]{0,1:T(8,128)S(1)} %bitcast.158, f32[256,768]{0,1:T(8,128)} %bitcast.159, f32[256,768]{0,1:T(8,128)} %bitcast.162, f32[768]{0:T(1024)S(1)} %fusion.95), kind=kOutput, calls=%fused_computation.43 | convolution fusion | flops 1817837568 | bytes 9440256 | tf_op jit(solution)/shard_map/fe,de->fd/dot_general | solution.py:126
  410.2 11.7 %fusion.140 = (f32[768]{0:T(1024)S(1)}, f32[768]{0:T(1024)S(1)}, f32[768,1536]{1,0:T(8,128)S(1)}) fusion(f32[768]{0:T(1024)S(1)} %add_rsqrt_fusion, f32[768]{0:T(1024)S(1)} %broadcast_multiply_fusion.2, bf16[768,1536]{1,0:T(8,128)(2,1)S(1)} %copy-done, bf16[1536,2304]{1,0:T(8,128)(2,1)} %all-gather.5.cloned.1.call-done, bf16[768,1536]{0,1:T(8,128)(2,1)} %fusion.66, ...), kind=kOutput, calls=%fused_computation.208 | convolution fusion | flops 5457049600 | bytes 17707008 | tf_op jit(solution)/shard_map/fe,de->fd/dot_general | solution.py:184
  421.9 2.8 fusion.21
  424.8 70.1 %reduce-scatter.5.cloned.1.call-done = bf16[96,2304]{1,0:T(8,128)(2,1)} async-done(((bf16[1536,2304]{1,0:T(8,128)(2,1)}), bf16[96,2304]{1,0:T(8,128)(2,1)}) %reduce-scatter.5.cloned.1.call-update) | async-done | bytes 442384 | tf_op jit(solution)/shard_map/reduce_scatter | solution.py:176
  (142 shorter events, 57.9 us)
Async XLA Ops:
  7.2 199.1 %all-gather.3.cloned.1.call-start = ((), (), s32[]{:S(2)}) async-start(), calls=%async_computation.2 | async-start | bytes 2506752 | tf_op jit(solution)/shard_map/all_gather | solution.py:129
  10.0 99.6 %copy-start.3 = (bf16[96,2304]{1,0:T(8,128)(2,1)}, bf16[96,2304]{1,0:T(8,128)(2,1)S(1)}, u32[]{:S(2)}) copy-start(bf16[96,2304]{1,0:T(8,128)(2,1)S(1)} %constant_dynamic-update-slice_fusion) | copy-start | bytes 1327108
  10.0 11.5 %collective-permute-start = (bf16[96,2304]{1,0:T(8,128)(2,1)S(1)}, bf16[96,2304]{1,0:T(8,128)(2,1)S(1)}, u32[]{:S(2)}, u32[]{:S(2)}) collective-permute-start(bf16[96,2304]{1,0:T(8,128)(2,1)S(1)} %constant_dynamic-update-slice_fusion), channel_id=1, source_target_pairs={{0,1},{1,2},{2,3},{3,4},{4,5},{5,6},{6,7},{7,8},{8,9},{9,10},{10,1... | collective-permute-start | bytes 1327112 | tf_op jit(solution)/shard_map/ppermute | solution.py:70
  21.5 10.5 %collective-permute-start.1 = (bf16[96,2304]{1,0:T(8,128)(2,1)S(1)}, bf16[96,2304]{1,0:T(8,128)(2,1)S(1)}, u32[]{:S(2)}, u32[]{:S(2)}) collective-permute-start(bf16[96,2304]{1,0:T(8,128)(2,1)S(1)} %collective-permute-done), channel_id=1, source_target_pairs={{0,1},{1,2},{2,3},{3,4},{4,5},{5,6},{6,7},{7,8},{8,9},{9,10},{10,1... | collective-permute-start | bytes 1327112 | tf_op jit(solution)/shard_map/ppermute | solution.py:70
  21.5 10.6 %collective-permute-start.8 = (bf16[96,2304]{1,0:T(8,128)(2,1)S(1)}, bf16[96,2304]{1,0:T(8,128)(2,1)S(1)}, u32[]{:S(2)}, u32[]{:S(2)}) collective-permute-start(bf16[96,2304]{1,0:T(8,128)(2,1)S(1)} %constant_dynamic-update-slice_fusion), channel_id=1, source_target_pairs={{1,0},{2,1},{3,2},{4,3},{5,4},{6,5},{7,6},{8,7},{9,8},{10,9},{11,1... | collective-permute-start | bytes 1327112 | tf_op jit(solution)/shard_map/ppermute | solution.py:74
  25.9 382.3 %reduce-scatter.7.cloned.1.call-start = ((), (), s32[]{:S(2)}) async-start(), calls=%async_computation.5 | async-start | bytes 2506752
  32.0 14.7 %collective-permute-start.2 = (bf16[96,2304]{1,0:T(8,128)(2,1)S(1)}, bf16[96,2304]{1,0:T(8,128)(2,1)S(1)}, u32[]{:S(2)}, u32[]{:S(2)}) collective-permute-start(bf16[96,2304]{1,0:T(8,128)(2,1)S(1)} %collective-permute-done.1), channel_id=1, source_target_pairs={{0,1},{1,2},{2,3},{3,4},{4,5},{5,6},{6,7},{7,8},{8,9},{9,10},{10,1... | collective-permute-start | bytes 1327112 | tf_op jit(solution)/shard_map/ppermute | solution.py:70
  32.1 14.7 %collective-permute-start.9 = (bf16[96,2304]{1,0:T(8,128)(2,1)S(1)}, bf16[96,2304]{1,0:T(8,128)(2,1)S(1)}, u32[]{:S(2)}, u32[]{:S(2)}) collective-permute-start(bf16[96,2304]{1,0:T(8,128)(2,1)S(1)} %collective-permute-done.8), channel_id=1, source_target_pairs={{1,0},{2,1},{3,2},{4,3},{5,4},{6,5},{7,6},{8,7},{9,8},{10,9},{11,1... | collective-permute-start | bytes 1327112 | tf_op jit(solution)/shard_map/ppermute | solution.py:74
  46.7 10.7 %collective-permute-start.3 = (bf16[96,2304]{1,0:T(8,128)(2,1)S(1)}, bf16[96,2304]{1,0:T(8,128)(2,1)S(1)}, u32[]{:S(2)}, u32[]{:S(2)}) collective-permute-start(bf16[96,2304]{1,0:T(8,128)(2,1)S(1)} %collective-permute-done.2), channel_id=1, source_target_pairs={{0,1},{1,2},{2,3},{3,4},{4,5},{5,6},{6,7},{7,8},{8,9},{9,10},{10,1... | collective-permute-start | bytes 1327112 | tf_op jit(solution)/shard_map/ppermute | solution.py:70
  46.8 17.9 %collective-permute-start.10 = (bf16[96,2304]{1,0:T(8,128)(2,1)S(1)}, bf16[96,2304]{1,0:T(8,128)(2,1)S(1)}, u32[]{:S(2)}, u32[]{:S(2)}) collective-permute-start(bf16[96,2304]{1,0:T(8,128)(2,1)S(1)} %collective-permute-done.9), channel_id=1, source_target_pairs={{1,0},{2,1},{3,2},{4,3},{5,4},{6,5},{7,6},{8,7},{9,8},{10,9},{11,1... | collective-permute-start | bytes 1327112 | tf_op jit(solution)/shard_map/ppermute | solution.py:74
  57.4 11.0 %collective-permute-start.4 = (bf16[96,2304]{1,0:T(8,128)(2,1)S(1)}, bf16[96,2304]{1,0:T(8,128)(2,1)S(1)}, u32[]{:S(2)}, u32[]{:S(2)}) collective-permute-start(bf16[96,2304]{1,0:T(8,128)(2,1)S(1)} %collective-permute-done.3), channel_id=1, source_target_pairs={{0,1},{1,2},{2,3},{3,4},{4,5},{5,6},{6,7},{7,8},{8,9},{9,10},{10,1... | collective-permute-start | bytes 1327112 | tf_op jit(solution)/shard_map/ppermute | solution.py:70
  64.6 9.1 %collective-permute-start.11 = (bf16[96,2304]{1,0:T(8,128)(2,1)S(1)}, bf16[96,2304]{1,0:T(8,128)(2,1)S(1)}, u32[]{:S(2)}, u32[]{:S(2)}) collective-permute-start(bf16[96,2304]{1,0:T(8,128)(2,1)S(1)} %collective-permute-done.10), channel_id=1, source_target_pairs={{1,0},{2,1},{3,2},{4,3},{5,4},{6,5},{7,6},{8,7},{9,8},{10,9},{11,1... | collective-permute-start | bytes 1327112 | tf_op jit(solution)/shard_map/ppermute | solution.py:74
  68.4 12.6 %collective-permute-start.5 = (bf16[96,2304]{1,0:T(8,128)(2,1)S(1)}, bf16[96,2304]{1,0:T(8,128)(2,1)S(1)}, u32[]{:S(2)}, u32[]{:S(2)}) collective-permute-start(bf16[96,2304]{1,0:T(8,128)(2,1)S(1)} %collective-permute-done.4), channel_id=1, source_target_pairs={{0,1},{1,2},{2,3},{3,4},{4,5},{5,6},{6,7},{7,8},{8,9},{9,10},{10,1... | collective-permute-start | bytes 1327112 | tf_op jit(solution)/shard_map/ppermute | solution.py:70
  73.7 14.1 %collective-permute-start.12 = (bf16[96,2304]{1,0:T(8,128)(2,1)S(1)}, bf16[96,2304]{1,0:T(8,128)(2,1)S(1)}, u32[]{:S(2)}, u32[]{:S(2)}) collective-permute-start(bf16[96,2304]{1,0:T(8,128)(2,1)S(1)} %collective-permute-done.11), channel_id=1, source_target_pairs={{1,0},{2,1},{3,2},{4,3},{5,4},{6,5},{7,6},{8,7},{9,8},{10,9},{11,1... | collective-permute-start | bytes 1327112 | tf_op jit(solution)/shard_map/ppermute | solution.py:74
  81.0 10.4 %collective-permute-start.6 = (bf16[96,2304]{1,0:T(8,128)(2,1)S(1)}, bf16[96,2304]{1,0:T(8,128)(2,1)S(1)}, u32[]{:S(2)}, u32[]{:S(2)}) collective-permute-start(bf16[96,2304]{1,0:T(8,128)(2,1)S(1)} %collective-permute-done.5), channel_id=1, source_target_pairs={{0,1},{1,2},{2,3},{3,4},{4,5},{5,6},{6,7},{7,8},{8,9},{9,10},{10,1... | collective-permute-start | bytes 1327112 | tf_op jit(solution)/shard_map/ppermute | solution.py:70
  87.8 10.9 %collective-permute-start.13 = (bf16[96,2304]{1,0:T(8,128)(2,1)S(1)}, bf16[96,2304]{1,0:T(8,128)(2,1)S(1)}, u32[]{:S(2)}, u32[]{:S(2)}) collective-permute-start(bf16[96,2304]{1,0:T(8,128)(2,1)S(1)} %collective-permute-done.12), channel_id=1, source_target_pairs={{1,0},{2,1},{3,2},{4,3},{5,4},{6,5},{7,6},{8,7},{9,8},{10,9},{11,1... | collective-permute-start | bytes 1327112 | tf_op jit(solution)/shard_map/ppermute | solution.py:74
  91.5 10.9 %collective-permute-start.7 = (bf16[96,2304]{1,0:T(8,128)(2,1)S(1)}, bf16[96,2304]{1,0:T(8,128)(2,1)S(1)}, u32[]{:S(2)}, u32[]{:S(2)}) collective-permute-start(bf16[96,2304]{1,0:T(8,128)(2,1)S(1)} %collective-permute-done.6), channel_id=1, source_target_pairs={{0,1},{1,2},{2,3},{3,4},{4,5},{5,6},{6,7},{7,8},{8,9},{9,10},{10,1... | collective-permute-start | bytes 1327112 | tf_op jit(solution)/shard_map/ppermute | solution.py:70
  98.7 15.7 %collective-permute-start.14 = (bf16[96,2304]{1,0:T(8,128)(2,1)S(1)}, bf16[96,2304]{1,0:T(8,128)(2,1)S(1)}, u32[]{:S(2)}, u32[]{:S(2)}) collective-permute-start(bf16[96,2304]{1,0:T(8,128)(2,1)S(1)} %collective-permute-done.13), channel_id=1, source_target_pairs={{1,0},{2,1},{3,2},{4,3},{5,4},{6,5},{7,6},{8,7},{9,8},{10,9},{11,1... | collective-permute-start | bytes 1327112 | tf_op jit(solution)/shard_map/ppermute | solution.py:74
  115.2 7.1 %copy-start = (bf16[768,1536]{1,0:T(8,128)(2,1)S(1)}, bf16[768,1536]{1,0:T(8,128)(2,1)}, u32[]{:S(2)}) copy-start(bf16[768,1536]{1,0:T(8,128)(2,1)} %param.15) | copy-start | bytes 7077892
  131.5 3.8 copy-start.1
  135.2 43.9 %collective-permute-start.15 = (bf16[256,1536]{1,0:T(8,128)(2,1)}, bf16[256,1536]{1,0:T(8,128)(2,1)}, u32[]{:S(2)}, u32[]{:S(2)}) collective-permute-start(bf16[256,1536]{1,0:T(8,128)(2,1)} %slice.184), channel_id=1, source_target_pairs={{0,1},{1,2},{2,3},{3,4},{4,5},{5,6},{6,7},{7,8},{8,9},{9,10},{10,1... | collective-permute-start | bytes 2359304 | tf_op jit(solution)/shard_map/ppermute | solution.py:25
  156.6 8.2 %copy-start.14 = (bf16[256,768]{0,1:T(8,128)(2,1)S(1)}, bf16[256,768]{0,1:T(8,128)(2,1)}, u32[]{:S(2)}) copy-start(bf16[256,768]{0,1:T(8,128)(2,1)} %copy.46) | copy-start | bytes 1179652
  171.5 5.2 %copy-start.19 = (f32[12,256,512]{2,1,0:T(8,128)S(1)}, f32[12,256,512]{2,1,0:T(8,128)}, u32[]{:S(2)}) copy-start(f32[12,256,512]{2,1,0:T(8,128)} %get-tuple-element.94) | copy-start | bytes 18874372
  171.5 5.2 %copy-start.20 = (f32[12,256]{1,0:T(8,128)S(1)}, f32[12,256]{1,0:T(8,128)}, u32[]{:S(2)}) copy-start(f32[12,256]{1,0:T(8,128)} %get-tuple-element.93) | copy-start | bytes 36868
  176.7 2.4 slice-start
  179.1 7.0 %copy-start.13 = (bf16[256,768]{0,1:T(8,128)(2,1)S(1)}, bf16[256,768]{0,1:T(8,128)(2,1)}, u32[]{:S(2)}) copy-start(bf16[256,768]{0,1:T(8,128)(2,1)} %copy.43) | copy-start | bytes 1179652
  192.8 4.9 copy-start.4
  192.8 4.9 copy-start.15
  192.8 4.9 copy-start.17
  196.8 0.9 copy-start.18
  205.4 204.7 %all-gather.5.cloned.1.call-start = ((), (), s32[]{:S(2)}) async-start(), calls=%async_computation.3 | async-start | bytes 7520256 | tf_op jit(solution)/shard_map/all_gather | solution.py:187
  206.2 288.6 %reduce-scatter.5.cloned.1.call-start = ((), (), s32[]{:S(2)}) async-start(), calls=%async_computation.4 | async-start | bytes 7520256 | tf_op jit(solution)/shard_map/reduce_scatter | solution.py:176
  206.2 5.5 %copy-start.2 = (bf16[512,768]{0,1:T(8,128)(2,1)S(1)}, bf16[512,768]{0,1:T(8,128)(2,1)}, u32[]{:S(2)}) copy-start(bf16[512,768]{0,1:T(8,128)(2,1)} %copy.48) | copy-start | bytes 2359300
  272.2 23.3 %copy-start.7 = (bf16[256,768]{0,1:T(8,128)(2,1)S(1)}, bf16[256,768]{0,1:T(8,128)(2,1)}, u32[]{:S(2)}) copy-start(bf16[256,768]{0,1:T(8,128)(2,1)} %get-tuple-element.87) | copy-start | bytes 1179652
  272.2 23.3 %copy-start.23 = (f32[12,256]{1,0:T(8,128)S(1)}, f32[12,256]{1,0:T(8,128)}, u32[]{:S(2)}) copy-start(f32[12,256]{1,0:T(8,128)} %get-tuple-element.95) | copy-start | bytes 36868
  295.5 3.5 copy-start.9
  299.0 1.0 copy-start.6
  299.0 1.0 copy-start.21
  299.0 6.8 %slice-start.1 = ((s8[6291456]{0:T(1024)(128)(4,1)}), s8[4194304]{0:T(1024)(128)(4,1)S(1)}, s32[]{:S(2)}) async-start(s8[6291456]{0:T(1024)(128)(4,1)} %bitcast.169), calls=%async_computation.7 | async-start | bytes 8388608
  300.0 4.8 copy-start.10
  300.0 5.8 %slice-start.2 = ((s8[6291456]{0:T(1024)(128)(4,1)}), s8[2097152]{0:T(1024)(128)(4,1)S(1)}, s32[]{:S(2)}) async-start(s8[6291456]{0:T(1024)(128)(4,1)} %bitcast.169), calls=%async_computation.8 | async-start | bytes 4194304
  304.8 1.0 copy-start.22
  305.8 1.7 copy-start.8
  310.4 4.0 copy-start.12
  311.4 76.4 %collective-permute-start.16 = (bf16[256,1536]{0,1:T(8,128)(2,1)}, bf16[256,1536]{0,1:T(8,128)(2,1)}, u32[]{:S(2)}, u32[]{:S(2)}) collective-permute-start(bf16[256,1536]{0,1:T(8,128)(2,1)} %slice.212), channel_id=1, source_target_pairs={{1,0},{2,1},{3,2},{4,3},{5,4},{6,5},{7,6},{8,7},{9,8},{10,9},{11,1... | collective-permute-start | bytes 2359304 | tf_op jit(solution)/shard_map/ppermute | solution.py:25
  339.3 22.7 %copy-start.11 = (bf16[512,768]{0,1:T(8,128)(2,1)S(1)}, bf16[512,768]{0,1:T(8,128)(2,1)}, u32[]{:S(2)}) copy-start(bf16[512,768]{0,1:T(8,128)(2,1)} %copy.47) | copy-start | bytes 2359300
  401.5 1.1 copy-start.16
  410.2 11.8 %copy-start.5 = (bf16[768,1536]{1,0:T(8,128)(2,1)S(1)}, bf16[768,1536]{1,0:T(8,128)(2,1)}, u32[]{:S(2)}) copy-start(bf16[768,1536]{1,0:T(8,128)(2,1)} %param.20) | copy-start | bytes 7077892
Sparse Core Ops, SparseCore 0:
  26.1 50.4 all-gather.2
  205.6 64.1 reduce-scatter.6
  272.3 70.5 all-gather.4
  401.6 93.1 reduce-scatter.4
